TPU v7x, 256 devices: a whole 4x4x8 slice. The times are simulated.
256 devices in a mesh: rep: 32 (over x, y, core), tp: 8 (over z).
Axes of the slice: x: 4, y: 4, z: 8, core: 2. Of those that a mesh axis runs over, the one named last changes fastest.
Arguments:
- hidden_in: bfloat16 [3072, 8192], P('rep', 'tp'), may hold values from -6 to 6
- queries: bfloat16 [3072, 8192], P('rep', 'tp'), may hold values from -20 to 20
- cache_keys: bfloat16 [3072, 128, 1024], P('rep', None, 'tp'), may hold values from -6 to 6
- cached_value_rows: bfloat16 [3072, 128, 1024], P('rep', None, 'tp'), may hold values from -6 to 6
- cache_lengths: int32 [3072], P('rep'), may hold values from 1 to 128, 98304 in all
- base_key_matrix: bfloat16 [8192, 1024], P(None, 'tp'), may hold values from -0.0625 to 0.0625
- base_value_matrix: bfloat16 [8192, 1024], P(None, 'tp'), may hold values from -0.0625 to 0.0625
- shrink_weights: bfloat16 [128, 8192, 128], P('rep', 'tp'), may hold values from -0.0625 to 0.0625
- pooled_up_weights: bfloat16 [128, 2, 64, 1024], P('rep', None, None, 'tp'), may hold values from -0.75 to 0.75
- block_owner: int32 [768, 1], P('rep'), may hold values from 0 to 31; in each aligned block of 24 rows (0 to 23, 24 to 47, ...) at most 2 rows name the same one
- block_slot: int32 [768], P('rep'), may hold values from 0 to 3
Outputs:
- new_keys: bfloat16 [3072, 1024], P('rep', 'tp')
- new_values: bfloat16 [3072, 1024], P('rep', 'tp')
- context: bfloat16 [3072, 8192], P('rep', 'tp')
Inputs may be any that keep to these rules, and one draw needn't show every extreme that they name: `block_owner`: among the 24 blocks of one replica group at most 2 name the same owner, and some group in every draw has 2 blocks with one owner.
All inputs are finite; a program needn't handle non-finite values. No bound on the sum of `cache_lengths` on one device may be relied on, other than what follows from the above.
Results may differ from a plain program's by a relative error of at most 0.0055.
Values may be sent and summed in bfloat16 or wider, within the bound.
A program may use at most 128 MiB of HBM per device.

v0:
```python
import jax
import jax.numpy as jnp
from jax import lax
from jax.sharding import PartitionSpec as P

HEAD_SIZE = 128
BLK = 4


adapter_scale = 0.5
masked_score = -1e30


def attend(group_queries, key_cache, value_cache, lengths, fresh_keys, fresh_values):
    rows_here = group_queries.shape[0]
    head_groups = key_cache.shape[2] // HEAD_SIZE
    group_size = group_queries.shape[1] // (head_groups * HEAD_SIZE)
    window = key_cache.shape[1]
    inverse_root = HEAD_SIZE ** (-0.5)
    query_heads = group_queries.reshape(rows_here, head_groups, group_size, HEAD_SIZE)
    key_heads = key_cache.reshape(rows_here, window, head_groups, HEAD_SIZE)
    value_heads = value_cache.reshape(rows_here, window, head_groups, HEAD_SIZE)
    scores = (
        jnp.einsum("rkgd,rtkd->rkgt", query_heads, key_heads, preferred_element_type=jnp.float32)
        * inverse_root
    )
    own_score = (
        jnp.einsum(
            "rkgd,rkd->rkg",
            query_heads,
            fresh_keys.reshape(rows_here, head_groups, HEAD_SIZE),
            preferred_element_type=jnp.float32,
        )
        * inverse_root
    )
    visible = (jnp.arange(window, dtype=jnp.int32)[None, :] < lengths[:, None])[:, None, None, :]
    highest = jnp.maximum(jnp.max(jnp.where(visible, scores, masked_score), axis=-1), own_score)
    exp_terms = jnp.where(visible, jnp.exp(scores - highest[..., None]), 0.0)
    own_term = jnp.exp(own_score - highest)
    denominator = jnp.sum(exp_terms, axis=-1) + own_term
    weights = (exp_terms / denominator[..., None]).astype(jnp.bfloat16)
    own_weight = (own_term / denominator).astype(jnp.bfloat16)
    context = jnp.einsum(
        "rkgt,rtkd->rkgd", weights, value_heads, preferred_element_type=jnp.float32
    )
    context = context + own_weight.astype(jnp.float32)[..., None] * fresh_values.reshape(
        rows_here, head_groups, 1, HEAD_SIZE
    ).astype(jnp.float32)
    return context.reshape(rows_here, -1).astype(jnp.bfloat16)


def earlier_ranks(owners):
    span_count = owners.shape[-1]
    matching = owners[..., :, None] == owners[..., None, :]
    before = jnp.arange(span_count)[:, None] > jnp.arange(span_count)[None, :]
    return jnp.sum((matching & before).astype(jnp.int32), axis=-1)


def slot_layout(owners_all, slots_all, myself, replicas, blocks_here, capacity):
    owners_grid = owners_all.reshape(replicas, blocks_here)
    slots_grid = slots_all.reshape(replicas, blocks_here)
    ranks_grid = earlier_ranks(owners_grid)
    placed = (owners_grid == myself)[:, :, None] & (
        ranks_grid[:, :, None] == jnp.arange(capacity, dtype=jnp.int32)[None, None, :]
    )
    placed_int = placed.astype(jnp.int32)
    slot_index = jnp.sum(placed_int * slots_grid[:, :, None], axis=1).reshape(replicas * capacity)
    return (placed, slot_index)


def adapter_pass(slot_rows, slot_index, shrink_weights, pooled_up_weights, site_sum):
    chosen_shrink = jnp.take(shrink_weights, slot_index, axis=0)
    selected_expand = jnp.take(pooled_up_weights, slot_index, axis=0)
    partial_value = jnp.einsum(
        "snd,sdr->snr", slot_rows, chosen_shrink, preferred_element_type=jnp.float32
    )
    shrunk = site_sum(partial_value).astype(jnp.bfloat16)
    split_halves = shrunk.reshape(shrunk.shape[0], shrunk.shape[1], 2, shrunk.shape[2] // 2)
    summed_terms = jnp.einsum(
        "snkr,skrw->snkw", split_halves, selected_expand, preferred_element_type=jnp.float32
    )
    return (adapter_scale * summed_terms).astype(jnp.bfloat16)


def shards(
    hidden_in,
    queries,
    cache_keys,
    cached_value_rows,
    cache_lengths,
    base_key_matrix,
    base_value_matrix,
    shrink_weights,
    pooled_up_weights,
    block_owner,
    block_slot,
):
    rows_here = hidden_in.shape[0]
    shard_width = hidden_in.shape[1]
    replicas = lax.axis_size("rep")
    myself = lax.axis_index("rep")
    blocks_here = rows_here // BLK
    capacity = max(2, (2 * blocks_here + replicas - 1) // replicas)
    key_row_width = base_key_matrix.shape[1]
    gathered = lax.all_gather(hidden_in, "tp", axis=1, tiled=True)
    base_keys = jnp.dot(gathered, base_key_matrix, preferred_element_type=jnp.float32)
    base_values = jnp.dot(gathered, base_value_matrix, preferred_element_type=jnp.float32)
    owners_all, slots_all = (
        lax.all_gather(block_owner[:, 0], "rep", axis=0, tiled=True),
        lax.all_gather(block_slot, "rep", axis=0, tiled=True),
    )
    placed, slot_index = slot_layout(owners_all, slots_all, myself, replicas, blocks_here, capacity)
    every_row = lax.all_gather(hidden_in, "rep", axis=0, tiled=True)
    same_group = jnp.eye(replicas, dtype=jnp.bfloat16)
    compactor = jnp.einsum("pq,qbc->pcqb", same_group, placed.astype(jnp.bfloat16)).reshape(
        replicas * capacity, replicas * blocks_here
    )
    slot_rows = jnp.dot(
        compactor,
        every_row.reshape(replicas * blocks_here, BLK * shard_width),
        preferred_element_type=jnp.float32,
    ).astype(jnp.bfloat16)
    slot_rows = slot_rows.reshape(replicas * capacity, BLK, shard_width)

    def sum_every(partial_value):
        return lax.psum(partial_value, "tp")

    deltas = adapter_pass(slot_rows, slot_index, shrink_weights, pooled_up_weights, sum_every)
    spread = jnp.einsum(
        "sq,sx->qx",
        compactor,
        deltas.reshape(replicas * capacity, BLK * 2 * key_row_width),
        preferred_element_type=jnp.float32,
    )
    spread = spread.reshape(replicas * rows_here, 2, key_row_width)
    per_row_delta = lax.psum_scatter(
        spread.astype(jnp.bfloat16), "rep", scatter_dimension=0, tiled=True
    ).astype(jnp.float32)
    fresh_keys = (base_keys + per_row_delta[:, 0]).astype(jnp.bfloat16)
    fresh_values = (base_values + per_row_delta[:, 1]).astype(jnp.bfloat16)
    context = attend(
        queries, cache_keys, cached_value_rows, cache_lengths, fresh_keys, fresh_values
    )
    return (fresh_keys, fresh_values, context)


def solution(mesh):
    return jax.shard_map(
        shards,
        mesh=mesh,
        in_specs=(
            P("rep", "tp"),
            P("rep", "tp"),
            P("rep", None, "tp"),
            P("rep", None, "tp"),
            P("rep"),
            P(None, "tp"),
            P(None, "tp"),
            P("rep", "tp", None),
            P("rep", None, None, "tp"),
            P("rep", None),
            P("rep"),
        ),
        out_specs=(P("rep", "tp"), P("rep", "tp"), P("rep", "tp")),
        check_vma=False,
    )
```

profile of v0, /device:TPU:1, one launch (start us, length us, event | category | flops | bytes accessed | tf_op | source)
XLA Modules:
  0.0 235.6 jit_solution(2521708871560459143)
XLA Ops:
  8.0 0.0 all-gather.6.cloned.1.call-start
  8.1 0.7 all-gather.6.cloned.1.call-update
  8.8 0.0 reduce-scatter.2.cloned.1.call-start
  8.8 1.4 dynamic-slice
  10.9 0.9 dynamic-update-slice.1
  11.8 0.7 bitcast_dynamic-update-slice_fusion
  12.5 14.7 %all-reduce.2 = (s32[768]{0:T(1024)S(1)}, s32[768]{0:T(1024)S(1)}) all-reduce(s32[768]{0:T(1024)S(1)} %bitcast_dynamic-update-slice_fusion, s32[768]{0:T(1024)S(1)} %dynamic-update-slice.1), channel_id=2, replica_groups=mesh['rep'=32,'tp'=8] {'rep'}, use_global_device_ids=true, to_apply=%add | all-reduce | flops 1536 | bytes 12288
  27.2 0.1 reshape.169
  27.3 0.1 copy.23
  27.3 0.2 convert_reduce_fusion
  27.5 0.1 copy.25
  27.6 0.1 mul.45
  27.7 0.1 select_reduce_fusion.1
  27.8 0.1 copy.26
  27.9 0.1 reshape.172
  28.0 0.1 reshape.171
  28.2 1.0 multiply_bitcast_fusion
  29.1 1.7 reshape.170
  30.9 2.1 gather_fusion
  33.0 8.6 %gather_fusion.1 = bf16[64,1024,128]{2,1,0:T(8,128)(2,1)} fusion(bf16[4,1024,128]{2,1,0:T(8,128)(2,1)} %param.18, s32[1024]{0:T(1024)S(1)} %pad_clamp_fusion), kind=kCustom, calls=%fused_computation.1 | custom fusion | bytes 33554688 | tf_op jit(solution)/shard_map/jit(_take)/gather | solution.py:72
  41.6 28.0 %all-gather.6.cloned.1.call-done = bf16[3072,1024]{1,0:T(8,128)(2,1)} async-done(((bf16[96,1024]{1,0:T(8,128)(2,1)}), bf16[3072,1024]{1,0:T(8,128)(2,1)}) %all-gather.6.cloned.1.call-update) | async-done | bytes 6291472 | tf_op jit(solution)/shard_map/all_gather | solution.py:113
  69.6 10.7 %reshape.173 = bf16[768,4096]{1,0:T(8,128)(2,1)} reshape(bf16[3072,1024]{1,0:T(8,128)(2,1)} %all-gather.6.cloned.1.call-done) | data formatting | bytes 12582912 | tf_op jit(solution)/shard_map/reshape | solution.py:120
  80.3 4.8 %convolution_convert_fusion = bf16[64,4096]{1,0:T(8,128)(2,1)} fusion(bf16[64,768]{1,0:T(8,128)(2,1)S(1)} %reshape.170, bf16[768,4096]{1,0:T(8,128)(2,1)} %reshape.173), kind=kOutput, calls=%fused_computation.6 | convolution fusion | flops 402915328 | bytes 6914048 | tf_op jit(solution)/shard_map/dot_general | solution.py:118
  85.1 2.2 reshape.174
  87.3 8.7 %fusion = f32[64,4,128]{2,1,0:T(4,128)S(1)} fusion(bf16[64,4,1024]{2,1,0:T(4,128)(2,1)} %reshape.174, bf16[64,1024,128]{2,1,0:T(8,128)(2,1)} %gather_fusion.1, pred[64]{0:T(512)(128)(4,1)S(1)} %compare_and_fusion), kind=kOutput, calls=%fused_computation.2 | convolution fusion | flops 75497472 | bytes 17432640 | tf_op jit(solution)/shard_map/snd,sdr->snr/dot_general | solution.py:74
  96.0 24.3 %all-reduce.4 = bf16[64,4,128]{2,1,0:T(4,128)(2,1)S(1)} all-reduce(f32[64,4,128]{2,1,0:T(4,128)S(1)} %fusion), channel_id=1, replica_groups=mesh['rep'=32,'tp'=8] {'tp'}, use_global_device_ids=true, to_apply=%region_2.3 | all-reduce | flops 32768 | bytes 196608 | tf_op jit(solution)/shard_map/psum | solution.py:126
  120.2 0.1 reshape.175
  120.4 2.3 fusion.14
  122.7 0.1 copy.29
  122.8 0.1 reshape.176
  122.9 1.8 convolution_convert_fusion.1
  124.6 3.8 %convert_element_type.61 = bf16[3072,2,128]{2,1,0:T(2,128)(2,1)} reshape(bf16[768,1024]{1,0:T(8,128)(2,1)} %convolution_convert_fusion.1) | data formatting | bytes 3145728 | tf_op jit(solution)/shard_map/convert_element_type | solution.py:137
  128.4 2.8 %copy.30 = bf16[3072,2,128]{2,0,1:T(8,128)(2,1)} copy(bf16[3072,2,128]{2,1,0:T(2,128)(2,1)} %convert_element_type.61) | data formatting | bytes 3145728 | tf_op jit(solution)/shard_map/convert_element_type | solution.py:137
  131.2 0.0 reduce-scatter.2.cloned.1.call-update
  131.3 0.2 all-gather.4.cloned.1.call-start
  131.5 0.3 all-gather.4.cloned.1.call-update
  131.9 0.1 iota_compare_fusion
  132.0 0.6 copy-done.4
  132.6 2.4 %select_reduce_fusion = (f32[96,8]{1,0:T(8,128)}, f32[96,8,128]{2,1,0:T(8,128)S(1)}) fusion(pred[96,128]{1,0:T(8,128)(4,1)S(1)} %iota_compare_fusion, bf16[96,8,128]{2,1,0:T(8,128)(2,1)S(1)} %bitcast.43, bf16[96,128,128]{2,1,0:T(8,128)(2,1)S(1)} %copy-done), kind=kOutput, calls=%fused_computation.25 | convolution fusion | flops 25459968 | bytes 3750912 | tf_op jit(solution)/shard_map/rkgd,rtkd->rkgt/dot_general | solution.py:24
  135.0 83.8 %reduce-scatter.2.cloned.1.call-done = bf16[96,2,128]{2,0,1:T(8,128)(2,1)} async-done(((bf16[3072,2,128]{2,0,1:T(8,128)(2,1)}), bf16[96,2,128]{2,0,1:T(8,128)(2,1)}) %reduce-scatter.2.cloned.1.call-update) | async-done | bytes 49168 | tf_op jit(solution)/shard_map/reduce_scatter | solution.py:136
  218.8 1.4 convert_element_type.62
  220.2 2.8 %fusion.17 = bf16[96,128]{1,0:T(8,128)(2,1)S(1)} fusion(bf16[96,8192]{1,0:T(8,128)(2,1)} %all-gather.4.cloned.1.call-done, bf16[8192,128]{1,0:T(8,128)(2,1)} %param.16, f32[96,2,128]{2,0,1:T(8,128)} %convert_element_type.62), kind=kOutput, calls=%fused_computation.19 | convolution fusion | flops 201351168 | bytes 3743744 | tf_op jit(solution)/shard_map/dot_general | solution.py:106
  223.0 1.2 fusion.26
  224.2 0.3 fusion.20
  224.6 1.2 fusion.38
  225.8 0.6 copy-done.10
  226.4 1.0 fusion.7
  227.4 0.7 copy.40
  (33 shorter events, 0.2 us)
Async XLA Ops:
  8.0 124.6 %copy-start = (bf16[96,128,128]{2,1,0:T(8,128)(2,1)S(1)}, bf16[96,128,128]{2,1,0:T(8,128)(2,1)}, u32[]{:S(2)}) copy-start(bf16[96,128,128]{2,1,0:T(8,128)(2,1)} %param.13) | copy-start | bytes 9437188
  8.0 22.8 %copy-start.1 = (bf16[4,2,64,128]{3,2,1,0:T(8,128)(2,1)S(1)}, bf16[4,2,64,128]{3,2,1,0:T(8,128)(2,1)}, u32[]{:S(2)}) copy-start(bf16[4,2,64,128]{3,2,1,0:T(8,128)(2,1)} %param.19) | copy-start | bytes 393220
  8.0 61.6 %all-gather.6.cloned.1.call-start = ((), (), s32[]{:S(2)}) async-start(), calls=%async_computation.2 | async-start | bytes 6488064 | tf_op jit(solution)/shard_map/all_gather | solution.py:113
  8.8 210.0 %reduce-scatter.2.cloned.1.call-start = ((), (), s32[]{:S(2)}) async-start(), calls=%async_computation.3 | async-start | bytes 1622016 | tf_op jit(solution)/shard_map/reduce_scatter | solution.py:136
  128.4 3.4 %copy-start.7 = (bf16[96,1024]{1,0:T(8,128)(2,1)S(1)}, bf16[96,1024]{1,0:T(8,128)(2,1)}, u32[]{:S(2)}) copy-start(bf16[96,1024]{1,0:T(8,128)(2,1)} %param.12) | copy-start | bytes 589828
  128.4 3.5 %copy-start.9 = (s32[96]{0:T(128)S(1)}, s32[96]{0:T(128)}, u32[]{:S(2)}) copy-start(s32[96]{0:T(128)} %param.15) | copy-start | bytes 1156
  131.3 89.0 %all-gather.4.cloned.1.call-start = ((), (), s32[]{:S(2)}) async-start(), calls=%async_computation.1 | async-start | bytes 1769472 | tf_op jit(solution)/shard_map/all_gather | solution.py:105
  131.9 0.7 copy-start.4
  220.2 4.0 %copy-start.5 = (f32[96,8]{1,0:T(8,128)S(1)}, f32[96,8]{1,0:T(8,128)}, u32[]{:S(2)}) copy-start(f32[96,8]{1,0:T(8,128)} %get-tuple-element.9) | copy-start | bytes 9220
  220.2 4.4 %copy-start.2 = (bf16[96,8192]{1,0:T(8,128)(2,1)S(1)}, bf16[96,8192]{1,0:T(8,128)(2,1)}, u32[]{:S(2)}) copy-start(bf16[96,8192]{1,0:T(8,128)(2,1)} %all-gather.4.cloned.1.call-done) | copy-start | bytes 4718596
  220.2 4.4 %copy-start.3 = (bf16[8192,128]{1,0:T(8,128)(2,1)S(1)}, bf16[8192,128]{1,0:T(8,128)(2,1)}, u32[]{:S(2)}) copy-start(bf16[8192,128]{1,0:T(8,128)(2,1)} %param.17) | copy-start | bytes 6291460
  220.2 4.4 %copy-start.6 = (f32[96,2,128]{2,0,1:T(8,128)S(1)}, f32[96,2,128]{2,0,1:T(8,128)}, u32[]{:S(2)}) copy-start(f32[96,2,128]{2,0,1:T(8,128)} %convert_element_type.62) | copy-start | bytes 294916
  223.0 2.8 %copy-start.8 = (bf16[96,128]{1,0:T(8,128)(2,1)}, bf16[96,128]{1,0:T(8,128)(2,1)S(1)}, u32[]{:S(2)}) copy-start(bf16[96,128]{1,0:T(8,128)(2,1)S(1)} %fusion.17) | copy-start | bytes 73732
  224.5 1.9 copy-start.10
Sparse Core Ops, SparseCore 0:
  11.4 58.1 all-gather.5
  131.4 87.3 reduce-scatter.1
Sparse Core Ops, SparseCore 1:
  133.5 38.5 all-gather.3
where the time goes:
time: 237 us; the launch traced here: 236 us
  waiting for transfers between devices  113 us (48%)
  blocking collectives  39 us (16%)
  local copies, waits for them, and re-layouts  37.9 us (16%)
  matrix products  26 us (11%)
  between operations  16.4 us (7%)
  other arithmetic  3.18 us (1%)
    reduce_scatter x1, waiting for transfers between devices, shards(): lax.psum_scatter(spread.astype(jnp.bfloat16), 'rep', scatter_dimension=0,...  83.8 us
    all_gather x1, waiting for transfers between devices, shards(): every_row = lax.all_gather(hidden_in, 'rep', axis=0, tiled=True)  28 us
    psum x1, blocking collectives, sum_every(): return lax.psum(partial_value, 'tp')  24.3 us
    unnamed x1, blocking collectives  14.7 us
    reshape x1, local copies, waits for them, and re-layouts, shards(): every_row.reshape(replicas * blocks_here, BLK * shard_width)  10.7 us
    dot_general x1, matrix products, adapter_pass(): jnp.einsum('snd,sdr->snr', slot_rows, chosen_shrink, preferred_element_ty...  8.66 us
    gather x1, local copies, waits for them, and re-layouts, adapter_pass(): chosen_shrink = jnp.take(shrink_weights, slot_index, axis=0)  8.59 us
    convert_element_type x2, local copies, waits for them, and re-layouts, shards(): spread.astype(jnp.bfloat16)  6.61 us
  transfers between devices with their start and end apart: 3, of which 2 were waited for; matrix products, arithmetic and copies ran while one was open for 9% of the time, Pallas kernels for 0%

commit v1 on v0

v1 whole, which is shorter than its diff:
```python
import functools
import jax
import jax.numpy as jnp
from jax import lax
from jax.experimental import pallas as pl
from jax.experimental.pallas import tpu as pltpu
from jax.sharding import PartitionSpec as P

HEAD_SIZE = 128
BLK = 4
CAP = 2
ADAPTER_SCALE = 0.5
MASKED = -1e30
MESH = pl.DeviceIdType.MESH
KV_CHUNKS = 4
UNROLL = 4


def kernel(
    N,
    T,
    lens_ref,
    owner_ref,
    slot_ref,
    hid_hbm,
    q_hbm,
    k_hbm,
    v_hbm,
    wk_hbm,
    wv_hbm,
    a_hbm,
    b_hbm,
    nk_ref,
    nv_ref,
    ctx_ref,
    hid,
    qin,
    kbuf,
    vbuf,
    wcat,
    acat,
    bcat,
    xbuf,
    sbuf,
    rbuf,
    part,
    prx,
    shr,
    srx,
    dsend,
    drx,
    qs,
    ms,
    ls,
    accs,
    base,
    load_sem,
    kv_sem,
    a2a_send,
    a2a_recv,
    ring_send,
    ring_recv,
    rs_send,
    rs_recv,
    ag_send,
    ag_recv,
    ret_send,
    ret_recv,
):
    f32, bf16 = jnp.float32, jnp.bfloat16
    R, D = hid.shape
    NB = R // BLK
    SL = CAP * BLK
    S = N * SL
    G = qin.shape[1] // HEAD_SIZE
    ADP = a_hbm.shape[0]
    RANK2 = a_hbm.shape[2]
    HALF = RANK2 // 2
    SG = S // T
    W = wk_hbm.shape[1]
    inverse_root = HEAD_SIZE ** (-0.5)
    me, z = lax.axis_index("rep"), lax.axis_index("tp")

    barrier = pltpu.get_barrier_semaphore()

    def greet_tp(i, c):
        pl.semaphore_signal(barrier, 1, device_id=(me, lax.rem(z + i, T)), device_id_type=MESH)
        return c

    def greet_rep(i, c):
        pl.semaphore_signal(barrier, 1, device_id=(lax.rem(me + i, N), z), device_id_type=MESH)
        return c

    lax.fori_loop(1, N, greet_rep, 0)
    lax.fori_loop(1, T, greet_tp, 0)

    load_hid = pltpu.make_async_copy(hid_hbm, hid, load_sem.at[0])
    load_q = pltpu.make_async_copy(q_hbm, qin, load_sem.at[1])
    load_hid.start()
    load_q.start()
    load_a = [
        pltpu.make_async_copy(
            a_hbm.at[j], acat.at[:, pl.ds(j * RANK2, RANK2)], load_sem.at[2 + j]
        )
        for j in range(ADP)
    ]
    load_w = [
        pltpu.make_async_copy(wk_hbm, wcat.at[:, pl.ds(0, W)], load_sem.at[2 + ADP]),
        pltpu.make_async_copy(wv_hbm, wcat.at[:, pl.ds(W, W)], load_sem.at[3 + ADP]),
    ]
    bcat[...] = jnp.zeros_like(bcat)
    load_b = [
        pltpu.make_async_copy(
            b_hbm.at[j, i],
            bcat.at[pl.ds(j * RANK2 + i * HALF, HALF), pl.ds(i * W, W)],
            load_sem.at[4 + ADP + 2 * j + i],
        )
        for j in range(ADP)
        for i in range(2)
    ]
    RC = R // KV_CHUNKS
    load_kv = [
        [
            pltpu.make_async_copy(
                src.at[pl.ds(c * RC, RC)], dst.at[pl.ds(c * RC, RC)], kv_sem.at[i, c]
            )
            for i, (src, dst) in enumerate(((k_hbm, kbuf), (v_hbm, vbuf)))
        ]
        for c in range(KV_CHUNKS)
    ]
    for pair in load_kv:
        for c in pair:
            c.start()
    for c in load_a:
        c.start()
    for c in load_w:
        c.start()

    lane = lax.broadcasted_iota(jnp.int32, (1, R), 1)
    block_of = lane // BLK
    owners = jnp.zeros((1, R), jnp.int32)
    slots = jnp.zeros((1, R), jnp.int32)
    for b in range(NB):
        owners = jnp.where(block_of == b, owner_ref[b], owners)
        slots = jnp.where(block_of == b, slot_ref[b], slots)
    ranks = jnp.zeros((1, R), jnp.int32)
    for b in range(NB):
        ranks = ranks + jnp.where((owners == owner_ref[b]) & (block_of > b), 1, 0)
    code = owners * SL + ranks * BLK + lane % BLK
    eye = lax.broadcasted_iota(jnp.int32, (R, R), 0) == lax.broadcasted_iota(jnp.int32, (R, R), 1)
    code_col = jnp.sum(jnp.where(eye, code.astype(f32), 0.0), axis=1, keepdims=True)
    slot_col = jnp.sum(jnp.where(eye, slots.astype(f32), 0.0), axis=1, keepdims=True)
    picks = (lax.broadcasted_iota(jnp.int32, (S, R), 0) == code).astype(bf16)
    one_hot = (
        lax.broadcasted_iota(jnp.int32, (R, 128), 1).astype(f32) == slot_col
    ).astype(bf16)
    load_hid.wait()
    sbuf[:, :, D:] = (
        jnp.dot(picks, one_hot, preferred_element_type=f32).reshape(N, SL, 128).astype(bf16)
    )
    for n in range(0, D, 256):
        sbuf[:, :, n : n + 256] = (
            jnp.dot(picks, hid[:, n : n + 256], preferred_element_type=f32)
            .reshape(N, SL, 256)
            .astype(bf16)
        )
    for c in load_b:
        c.start()

    def ring(direction, d, h, arriving):
        step = d if arriving else d - 1
        s = lax.rem(z + (T - step), T) if direction == 0 else lax.rem(z + step, T)
        to = lax.rem(z + 1, T) if direction == 0 else lax.rem(z + (T - 1), T)
        rows = pl.ds(h * (R // 2), R // 2)
        src = hid.at[rows] if d == 1 else xbuf.at[s, rows]
        return pltpu.make_async_remote_copy(
            src_ref=src,
            dst_ref=xbuf.at[s, rows],
            send_sem=ring_send.at[direction, d - 1, h],
            recv_sem=ring_recv.at[direction, d - 1, h],
            device_id=(me, to),
            device_id_type=MESH,
        )

    def carries(direction, d, h):
        return d < T // 2 or (d == T // 2 and h == direction)

    def a2a(i, arriving):
        peer = lax.rem(me + i, N)
        frm = peer if arriving else me
        return pltpu.make_async_remote_copy(
            src_ref=sbuf.at[peer],
            dst_ref=rbuf.at[frm],
            send_sem=a2a_send.at[peer],
            recv_sem=a2a_recv.at[frm],
            device_id=(peer, z),
            device_id_type=MESH,
        )

    def scatter(i, arriving):
        peer = lax.rem(z + i, T)
        frm = peer if arriving else z
        return pltpu.make_async_remote_copy(
            src_ref=part.at[peer],
            dst_ref=prx.at[frm],
            send_sem=rs_send.at[peer],
            recv_sem=rs_recv.at[frm],
            device_id=(me, peer),
            device_id_type=MESH,
        )

    def gather(i, arriving):
        peer = lax.rem(z + i, T)
        frm = peer if arriving else z
        return pltpu.make_async_remote_copy(
            src_ref=shr,
            dst_ref=srx.at[frm],
            send_sem=ag_send.at[peer],
            recv_sem=ag_recv.at[frm],
            device_id=(me, peer),
            device_id_type=MESH,
        )

    def give_back(i, arriving):
        peer = lax.rem(me + i, N)
        frm = peer if arriving else me
        return pltpu.make_async_remote_copy(
            src_ref=dsend.at[peer],
            dst_ref=drx.at[frm],
            send_sem=ret_send.at[peer],
            recv_sem=ret_recv.at[frm],
            device_id=(peer, z),
            device_id_type=MESH,
        )

    def loop(n, f):
        def step(i, c):
            f(i)
            return c

        lax.fori_loop(1, n, step, 0)

    def ring_events(d):
        for h in range(2):
            for direction in range(2):
                if carries(direction, d, h):
                    ring(direction, d, h, True).wait_recv()
                    if carries(direction, d + 1, h):
                        ring(direction, d + 1, h, False).start()

    def base_block(s, first=False):
        x = hid[...] if first else xbuf[s]
        y = jnp.dot(
            x, wcat[pl.ds(pl.multiple_of(s * D, D), D), :], preferred_element_type=f32
        )
        base[...] = y if first else base[...] + y

    def attend(chunk):
        for c in load_kv[chunk]:
            c.wait()
        position = lax.broadcasted_iota(jnp.int32, (G, k_hbm.shape[1]), 1)

        def step(i, carry):
            for u in range(UNROLL):
                r = chunk * RC + i * UNROLL + u
                q = qs[r].astype(bf16)
                s = lax.dot_general(
                    q, kbuf[r], (((1,), (1,)), ((), ())), preferred_element_type=f32
                )
                s = jnp.where(position < lens_ref[r], s * inverse_root, MASKED)
                m = jnp.max(s, axis=-1, keepdims=True)
                p = jnp.exp(s - m)
                l = jnp.sum(p, axis=-1, keepdims=True)
                accs[r] = jnp.dot(p.astype(bf16), vbuf[r], preferred_element_type=f32)
                ms[r] = jnp.broadcast_to(m, (G, HEAD_SIZE))
                ls[r] = jnp.broadcast_to(l, (G, HEAD_SIZE))
            return carry

        lax.fori_loop(0, RC // UNROLL, step, 0)

    pl.semaphore_wait(barrier, N - 1 + T - 1)
    for h in range(2):
        for direction in range(2):
            ring(direction, 1, h, False).start()
    loop(N, lambda i: a2a(i, False).start())
    rbuf[me] = sbuf[me]

    load_q.wait()
    for g in range(G):
        qs[:, g, :] = qin[:, g * HEAD_SIZE : (g + 1) * HEAD_SIZE].astype(f32)
    attend(0)
    ring_events(1)
    attend(1)
    ring_events(2)
    attend(2)
    loop(N, lambda i: a2a(i, True).wait_recv())

    for c in load_a:
        c.wait()
    rows = rbuf[...].astype(f32).reshape(S, D + 128).astype(bf16)
    y = jnp.dot(rows[:, :D], acat[...], preferred_element_type=f32)
    hot = rows[:, D:].astype(f32)
    partial = jnp.zeros((S, RANK2), f32)
    for j in range(ADP):
        partial = partial + y[:, j * RANK2 : (j + 1) * RANK2] * hot[:, j : j + 1]
    part[...] = partial.reshape(T, SG, RANK2)
    loop(T, lambda i: scatter(i, False).start())
    prx[z] = part[z]
    ring_events(3)
    for c in load_w:
        c.wait()
    base_block(z, True)
    attend(3)
    loop(T, lambda i: scatter(i, True).wait_recv())
    total = prx[0]
    for t in range(1, T):
        total = total + prx[t]
    shr[...] = total.astype(bf16)
    loop(T, lambda i: gather(i, False).start())
    srx[z] = shr[...]
    for d in range(1, T // 2):
        base_block(lax.rem(z + d, T))
        base_block(lax.rem(z + (T - d), T))
    loop(T, lambda i: gather(i, True).wait_recv())
    for c in load_b:
        c.wait()
    shrunk = srx[...].reshape(S, RANK2)
    masked = jnp.concatenate(
        [shrunk * hot[:, j : j + 1].astype(bf16) for j in range(ADP)], axis=1
    )
    delta = ADAPTER_SCALE * jnp.dot(masked, bcat[...], preferred_element_type=f32)
    dsend[...] = delta.reshape(N, SL, 2 * W).astype(bf16)
    loop(N, lambda i: give_back(i, False).start())
    drx[me] = dsend[me]
    ring_events(T // 2)
    base_block(lax.rem(z + T // 2, T))
    loop(N, lambda i: give_back(i, True).wait_recv())

    spread = (
        lax.broadcasted_iota(jnp.int32, (R, S), 1).astype(f32) == code_col
    ).astype(bf16)
    got = drx[...].astype(f32).reshape(S, 2 * W).astype(bf16)
    fresh = (base[...] + jnp.dot(spread, got, preferred_element_type=f32)).astype(bf16)
    nk_ref[...] = fresh[:, :W]
    nv_ref[...] = fresh[:, W:]
    fresh = fresh.astype(f32)
    base[...] = fresh
    nk = fresh[:, :W].reshape(R, 1, W)
    nv = fresh[:, W:].reshape(R, 1, W)
    own = jnp.sum(qs[...] * nk, axis=-1, keepdims=True) * inverse_root
    m_c = ms[...]
    top = jnp.maximum(m_c, own)
    a_c = jnp.exp(m_c - top)
    a_o = jnp.exp(own - top)
    inv = 1.0 / (ls[...] * a_c + a_o)
    w_o = (a_o * inv).astype(bf16).astype(f32)
    accs[...] = accs[...] * (a_c * inv) + w_o * nv
    for g in range(G):
        ctx_ref[:, g * HEAD_SIZE : (g + 1) * HEAD_SIZE] = accs[:, g, :].astype(bf16)

    for h in range(2):
        for direction in range(2):
            for d in range(1, T // 2 + 1):
                if carries(direction, d, h):
                    ring(direction, d, h, False).wait_send()
    loop(N, lambda i: a2a(i, False).wait_send())
    loop(T, lambda i: scatter(i, False).wait_send())
    loop(T, lambda i: gather(i, False).wait_send())
    loop(N, lambda i: give_back(i, False).wait_send())


def shards(
    hidden_in,
    queries,
    cache_keys,
    cached_value_rows,
    cache_lengths,
    base_key_matrix,
    base_value_matrix,
    shrink_weights,
    pooled_up_weights,
    block_owner,
    block_slot,
):
    N, T = lax.axis_size("rep"), lax.axis_size("tp")
    R, D = hidden_in.shape
    C = cache_keys.shape[1]
    W = base_key_matrix.shape[1]
    G = queries.shape[1] // HEAD_SIZE
    ADP, _, RANK2 = shrink_weights.shape
    SL = CAP * BLK
    S = N * SL
    f32, bf16 = jnp.float32, jnp.bfloat16
    smem = pl.BlockSpec(memory_space=pltpu.SMEM)
    hbm = pl.BlockSpec(memory_space=pl.ANY)
    vmem = pl.BlockSpec(memory_space=pltpu.VMEM)
    dma = pltpu.SemaphoreType.DMA
    return pl.pallas_call(
        functools.partial(kernel, N, T),
        out_shape=(
            jax.ShapeDtypeStruct((R, W), bf16),
            jax.ShapeDtypeStruct((R, W), bf16),
            jax.ShapeDtypeStruct((R, G * HEAD_SIZE), bf16),
        ),
        in_specs=[smem] * 3 + [hbm] * 8,
        out_specs=(vmem, vmem, vmem),
        scratch_shapes=[
            pltpu.VMEM((R, D), bf16),
            pltpu.VMEM((R, G * HEAD_SIZE), bf16),
            pltpu.VMEM((R, C, W), bf16),
            pltpu.VMEM((R, C, W), bf16),
            pltpu.VMEM((T * D, 2 * W), bf16),
            pltpu.VMEM((D, ADP * RANK2), bf16),
            pltpu.VMEM((ADP * RANK2, 2 * W), bf16),
            pltpu.VMEM((T, R, D), bf16),
            pltpu.VMEM((N, SL, D + 128), bf16),
            pltpu.VMEM((N, SL, D + 128), bf16),
            pltpu.VMEM((T, S // T, RANK2), f32),
            pltpu.VMEM((T, S // T, RANK2), f32),
            pltpu.VMEM((S // T, RANK2), bf16),
            pltpu.VMEM((T, S // T, RANK2), bf16),
            pltpu.VMEM((N, SL, 2 * W), bf16),
            pltpu.VMEM((N, SL, 2 * W), bf16),
            pltpu.VMEM((R, G, HEAD_SIZE), f32),
            pltpu.VMEM((R, G, HEAD_SIZE), f32),
            pltpu.VMEM((R, G, HEAD_SIZE), f32),
            pltpu.VMEM((R, G, HEAD_SIZE), f32),
            pltpu.VMEM((R, 2 * W), f32),
            dma((4 + 3 * ADP,)),
            dma((2, KV_CHUNKS)),
            dma((N,)),
            dma((N,)),
            dma((2, T // 2, 2)),
            dma((2, T // 2, 2)),
            dma((T,)),
            dma((T,)),
            dma((T,)),
            dma((T,)),
            dma((N,)),
            dma((N,)),
        ],
        compiler_params=pltpu.CompilerParams(
            collective_id=0, has_side_effects=True, vmem_limit_bytes=48 * 1024 * 1024
        ),
    )(
        cache_lengths,
        block_owner[:, 0],
        block_slot,
        hidden_in,
        queries,
        cache_keys,
        cached_value_rows,
        base_key_matrix,
        base_value_matrix,
        shrink_weights,
        pooled_up_weights,
    )


def solution(mesh):
    return jax.shard_map(
        shards,
        mesh=mesh,
        in_specs=(
            P("rep", "tp"),
            P("rep", "tp"),
            P("rep", None, "tp"),
            P("rep", None, "tp"),
            P("rep"),
            P(None, "tp"),
            P(None, "tp"),
            P("rep", "tp", None),
            P("rep", None, None, "tp"),
            P("rep", None),
            P("rep"),
        ),
        out_specs=(P("rep", "tp"), P("rep", "tp"), P("rep", "tp")),
        check_vma=False,
    )
```

time: 237 us -> 64.9 us (0.27)
  waiting for transfers between devices: 113 us -> 0 us
  Pallas kernels: 0 us -> 52.9 us
  blocking collectives: 39 us -> 0 us
  local copies, waits for them, and re-layouts: 37.9 us -> 11 us
  matrix products: 26 us -> 0 us
  between operations: 16.4 us -> 0.66 us
  other arithmetic: 3.18 us -> 0 us
    reduce_scatter x1 -> x0, waiting for transfers between devices: 83.8 us -> none  [shards(): lax.psum_scatter(spread.astype(jnp.bfloat16), 'rep', scatter_dimension=0,...]
    pallas_call x0 -> x1, Pallas kernels: none -> 52.9 us  [shards(): pl.pallas_call(functools.partial(kernel, N, T), out_shape=(jax.ShapeDtype...]
    all_gather x2 -> x0, waiting for transfers between devices: 28 us -> none  [the longest x1 28 us: shards(): every_row = lax.all_gather(hidden_in, 'rep', axis=0, tiled=True)]
    dot_general x9 -> x0, matrix products: 26 us -> none  [the longest x1 8.66 us: adapter_pass(): jnp.einsum('snd,sdr->snr', slot_rows, chosen_shrink, preferred_element_ty...]
    psum x1 -> x0, blocking collectives: 24.3 us -> none  [sum_every(): return lax.psum(partial_value, 'tp')]
    reshape x9 -> x0, local copies, waits for them, and re-layouts: 15.2 us -> none  [the longest x1 10.7 us: shards(): every_row.reshape(replicas * blocks_here, BLK * shard_width)]
    unnamed x1 -> x0, blocking collectives: 14.7 us -> none
    gather x2 -> x0, local copies, waits for them, and re-layouts: 10.7 us -> none  [the longest x1 8.59 us: adapter_pass(): chosen_shrink = jnp.take(shrink_weights, slot_index, axis=0)]
  transfers between devices with their start and end apart: 3 -> 0, of which waited for: 2 -> 0; matrix products, arithmetic and copies ran while one was open for 9% -> 0% of each run, Pallas kernels for 0% -> 0%
where the time goes in v1:
time: 64.9 us; the launch traced here: 64.6 us
  Pallas kernels  52.9 us (82%)
  local copies, waits for them, and re-layouts  11 us (17%)
  between operations  0.66 us (1%)
    pallas_call x1, Pallas kernels, shards(): pl.pallas_call(functools.partial(kernel, N, T), out_shape=(jax.ShapeDtype...  52.9 us
    unnamed x21, local copies, waits for them, and re-layouts  11 us

profile of v1, /device:TPU:1, one launch (start us, length us, event | category | flops | bytes accessed | tf_op | source)
XLA Modules:
  0.0 64.6 jit_solution(4364180675931457635)
XLA Ops:
  0.6 0.0 copy-start
  0.6 1.6 %copy-done = bf16[8192,128]{1,0:T(8,128)(2,1)S(1)} copy-done((bf16[8192,128]{1,0:T(8,128)(2,1)S(1)}, bf16[8192,128]{1,0:T(8,128)(2,1)}, u32[]{:S(2)}) %copy-start) | copy-done | bytes 2097176
  2.2 0.0 copy-start.1
  2.2 1.6 %copy-done.1 = bf16[8192,128]{1,0:T(8,128)(2,1)S(1)} copy-done((bf16[8192,128]{1,0:T(8,128)(2,1)S(1)}, bf16[8192,128]{1,0:T(8,128)(2,1)}, u32[]{:S(2)}) %copy-start.1) | copy-done | bytes 2097176
  3.8 0.0 copy-start.2
  3.8 1.2 %copy-done.2 = bf16[4,1024,128]{2,1,0:T(8,128)(2,1)S(1)} copy-done((bf16[4,1024,128]{2,1,0:T(8,128)(2,1)S(1)}, bf16[4,1024,128]{2,1,0:T(8,128)(2,1)}, u32[]{:S(2)}) %copy-start.2) | copy-done | bytes 1048600
  5.0 0.0 copy-start.3
  5.0 0.9 %copy-done.3 = bf16[96,1024]{1,0:T(8,128)(2,1)S(1)} copy-done((bf16[96,1024]{1,0:T(8,128)(2,1)S(1)}, bf16[96,1024]{1,0:T(8,128)(2,1)}, u32[]{:S(2)}) %copy-start.3) | copy-done | bytes 196632
  6.0 0.0 copy-start.4
  6.0 0.9 %copy-done.4 = bf16[96,1024]{1,0:T(8,128)(2,1)S(1)} copy-done((bf16[96,1024]{1,0:T(8,128)(2,1)S(1)}, bf16[96,1024]{1,0:T(8,128)(2,1)}, u32[]{:S(2)}) %copy-start.4) | copy-done | bytes 196632
  6.9 0.0 copy-start.5
  6.9 0.9 %copy-done.5 = bf16[4,2,64,128]{3,2,1,0:T(8,128)(2,1)S(1)} copy-done((bf16[4,2,64,128]{3,2,1,0:T(8,128)(2,1)S(1)}, bf16[4,2,64,128]{3,2,1,0:T(8,128)(2,1)}, u32[]{:S(2)}) %copy-start.5) | copy-done | bytes 131096
  7.8 0.0 copy-start.6
  7.8 0.7 %copy-done.6 = s32[96]{0:T(128)S(1)} copy-done((s32[96]{0:T(128)S(1)}, s32[96]{0:T(128)}, u32[]{:S(2)}) %copy-start.6) | copy-done | bytes 408
  8.5 0.0 copy-start.7
  8.5 0.7 %copy-done.7 = s32[24,1]{0,1:T(1,128)S(1)} copy-done((s32[24,1]{0,1:T(1,128)S(1)}, s32[24,1]{0,1:T(1,128)}, u32[]{:S(2)}) %copy-start.7) | copy-done | bytes 120
  9.1 0.0 copy-start.8
  9.1 0.7 %copy-done.8 = s32[24]{0:T(128)S(1)} copy-done((s32[24]{0:T(128)S(1)}, s32[24]{0:T(128)}, u32[]{:S(2)}) %copy-start.8) | copy-done | bytes 120
  9.8 52.9 %shard_map.130 = (bf16[96,128]{1,0:T(8,128)(2,1)S(1)}, bf16[96,128]{1,0:T(8,128)(2,1)S(1)}, bf16[96,1024]{1,0:T(8,128)(2,1)S(1)}) custom-call(s32[96]{0:T(128)S(1)} %copy-done.6, s32[24]{0:T(128)S(1)} %bitcast.1, s32[24]{0:T(128)S(1)} %copy-done.8, bf16[96,1024]{1,0:T(8,128)(2,1)S(1)} %copy-done.3, bf16[96,1024]{1,0:T(8,128)(2,1)S(1)} %copy-done.4, ...), custom_call_target="tpu_custom_call" | custom-call | tf_op jit(solution)/shard_map/pallas_call | solution.py:398
  62.7 0.6 copy.17
  63.3 0.6 copy.18
  63.9 0.7 %copy.19 = bf16[96,1024]{1,0:T(8,128)(2,1)} copy(bf16[96,1024]{1,0:T(8,128)(2,1)S(1)} %get-tuple-element.8) | data formatting | bytes 393216
Async XLA Ops:
  0.6 1.6 %copy-start = (bf16[8192,128]{1,0:T(8,128)(2,1)S(1)}, bf16[8192,128]{1,0:T(8,128)(2,1)}, u32[]{:S(2)}) copy-start(bf16[8192,128]{1,0:T(8,128)(2,1)} %wk_hbm.1) | copy-start | bytes 6291460
  2.2 1.6 %copy-start.1 = (bf16[8192,128]{1,0:T(8,128)(2,1)S(1)}, bf16[8192,128]{1,0:T(8,128)(2,1)}, u32[]{:S(2)}) copy-start(bf16[8192,128]{1,0:T(8,128)(2,1)} %wv_hbm.1) | copy-start | bytes 6291460
  3.8 1.2 %copy-start.2 = (bf16[4,1024,128]{2,1,0:T(8,128)(2,1)S(1)}, bf16[4,1024,128]{2,1,0:T(8,128)(2,1)}, u32[]{:S(2)}) copy-start(bf16[4,1024,128]{2,1,0:T(8,128)(2,1)} %a_hbm.1) | copy-start | bytes 3145732
  5.0 0.9 %copy-start.3 = (bf16[96,1024]{1,0:T(8,128)(2,1)S(1)}, bf16[96,1024]{1,0:T(8,128)(2,1)}, u32[]{:S(2)}) copy-start(bf16[96,1024]{1,0:T(8,128)(2,1)} %hid_hbm.1) | copy-start | bytes 589828
  6.0 0.9 %copy-start.4 = (bf16[96,1024]{1,0:T(8,128)(2,1)S(1)}, bf16[96,1024]{1,0:T(8,128)(2,1)}, u32[]{:S(2)}) copy-start(bf16[96,1024]{1,0:T(8,128)(2,1)} %q_hbm.1) | copy-start | bytes 589828
  6.9 0.9 %copy-start.5 = (bf16[4,2,64,128]{3,2,1,0:T(8,128)(2,1)S(1)}, bf16[4,2,64,128]{3,2,1,0:T(8,128)(2,1)}, u32[]{:S(2)}) copy-start(bf16[4,2,64,128]{3,2,1,0:T(8,128)(2,1)} %b_hbm.1) | copy-start | bytes 393220
  7.8 0.7 %copy-start.6 = (s32[96]{0:T(128)S(1)}, s32[96]{0:T(128)}, u32[]{:S(2)}) copy-start(s32[96]{0:T(128)} %lens_ref.1) | copy-start | bytes 1156
  8.5 0.7 %copy-start.7 = (s32[24,1]{0,1:T(1,128)S(1)}, s32[24,1]{0,1:T(1,128)}, u32[]{:S(2)}) copy-start(s32[24,1]{0,1:T(1,128)} %param.20) | copy-start | bytes 292
  9.1 0.7 %copy-start.8 = (s32[24]{0:T(128)S(1)}, s32[24]{0:T(128)}, u32[]{:S(2)}) copy-start(s32[24]{0:T(128)} %slot_ref.1) | copy-start | bytes 292

commit v2 on v1

v2 whole, which is shorter than its diff:
```python
import functools
import jax
import jax.numpy as jnp
from jax import lax
from jax.experimental import pallas as pl
from jax.experimental.pallas import tpu as pltpu
from jax.sharding import PartitionSpec as P

HEAD_SIZE = 128
BLK = 4
CAP = 2
ADAPTER_SCALE = 0.5
MASKED = -1e30
MESH = pl.DeviceIdType.MESH
KV_CHUNKS = 6
EARLY = 1
VMEM_LIMIT = 40 * 1024 * 1024


def kernel(
    N,
    T,
    lens_hbm,
    owner_hbm,
    slot_hbm,
    hid_hbm,
    q_hbm,
    k_hbm,
    v_hbm,
    wk_hbm,
    wv_hbm,
    a_hbm,
    b_hbm,
    nk_ref,
    nv_ref,
    ctx_ref,
    lens_ref,
    owner_ref,
    slot_ref,
    hid,
    qin,
    kbuf,
    vbuf,
    wcat,
    acat,
    bcat,
    xbuf,
    sbuf,
    rbuf,
    part,
    prx,
    shr,
    srx,
    dsend,
    drx,
    qs,
    ms,
    ls,
    accs,
    base,
    hot,
    load_sem,
    kv_sem,
    a2a_send,
    a2a_recv,
    ring_send,
    ring_recv,
    rs_sem,
    ag_sem,
    ret_sem,
):
    f32, bf16 = jnp.float32, jnp.bfloat16
    R, D = hid.shape
    NB = R // BLK
    SL = CAP * BLK
    S = N * SL
    G = qin.shape[1] // HEAD_SIZE
    ADP = a_hbm.shape[0]
    RANK2 = a_hbm.shape[2]
    HALF = RANK2 // 2
    SG = S // T
    W = wk_hbm.shape[1]
    inverse_root = HEAD_SIZE ** (-0.5)
    me, z = lax.axis_index("rep"), lax.axis_index("tp")

    barrier = pltpu.get_barrier_semaphore()

    NC, NY = 2, 4
    NX = N // (NC * NY)
    mc, my, mx = lax.rem(me, NC), lax.rem(me // NC, NY), me // (NC * NY)
    xs = [lax.rem(mx + i, NX) * (NC * NY) for i in range(NX)]
    ys = [lax.rem(my + i, NY) * NC for i in range(NY)]
    cs = [mc, 1 - mc]
    far = lambda n: sorted(range(n), key=lambda i: -min(i, n - i))
    rep_peers = [
        xs[i] + ys[j] + cs[k]
        for i, j, k in sorted(
            ((i, j, k) for i in range(NX) for j in range(NY) for k in range(NC)),
            key=lambda t: -(min(t[0], NX - t[0]) + min(t[1], NY - t[1])),
        )
        if (i, j, k) != (0, 0, 0)
    ]
    tp_peers = [lax.rem(z + i, T) for i in far(T) if i]
    load_hid = pltpu.make_async_copy(hid_hbm, hid, load_sem.at[0])
    load_q = pltpu.make_async_copy(q_hbm, qin, load_sem.at[1])
    load_ids = [
        pltpu.make_async_copy(owner_hbm, owner_ref, load_sem.at[4 + 3 * ADP]),
        pltpu.make_async_copy(slot_hbm, slot_ref, load_sem.at[5 + 3 * ADP]),
        pltpu.make_async_copy(lens_hbm, lens_ref, load_sem.at[6 + 3 * ADP]),
    ]
    load_hid.start()
    for c in load_ids:
        c.start()
    load_q.start()
    for p in tp_peers:
        pl.semaphore_signal(barrier, 1, device_id=(me, p), device_id_type=MESH)
    for p in rep_peers:
        pl.semaphore_signal(barrier, 1, device_id=(p, z), device_id_type=MESH)
    load_a = [
        pltpu.make_async_copy(
            a_hbm.at[j], acat.at[:, pl.ds(j * RANK2, RANK2)], load_sem.at[2 + j]
        )
        for j in range(ADP)
    ]
    load_w = [
        pltpu.make_async_copy(wk_hbm, wcat.at[:, pl.ds(0, W)], load_sem.at[2 + ADP]),
        pltpu.make_async_copy(wv_hbm, wcat.at[:, pl.ds(W, W)], load_sem.at[3 + ADP]),
    ]
    bcat[...] = jnp.zeros_like(bcat)
    load_b = [
        pltpu.make_async_copy(
            b_hbm.at[j, i],
            bcat.at[pl.ds(j * RANK2 + i * HALF, HALF), pl.ds(i * W, W)],
            load_sem.at[4 + ADP + 2 * j + i],
        )
        for j in range(ADP)
        for i in range(2)
    ]
    RC = R // KV_CHUNKS
    load_kv = [
        [
            pltpu.make_async_copy(
                src.at[pl.ds(c * RC, RC)], dst.at[pl.ds(c * RC, RC)], kv_sem.at[i, c]
            )
            for i, (src, dst) in enumerate(((k_hbm, kbuf), (v_hbm, vbuf)))
        ]
        for c in range(KV_CHUNKS)
    ]
    for pair in load_kv:
        for c in pair:
            c.start()
    for c in load_a:
        c.start()
    for c in load_w:
        c.start()

    lane = lax.broadcasted_iota(jnp.int32, (1, R), 1)
    block_of = lane // BLK
    for c in load_ids:
        c.wait()
    owners = jnp.zeros((1, R), jnp.int32)
    slots = jnp.zeros((1, R), jnp.int32)
    for b in range(NB):
        owners = jnp.where(block_of == b, owner_ref[b], owners)
        slots = jnp.where(block_of == b, slot_ref[b], slots)
    ranks = jnp.zeros((1, R), jnp.int32)
    for b in range(NB):
        ranks = ranks + jnp.where((owners == owner_ref[b]) & (block_of > b), 1, 0)
    code = owners * SL + ranks * BLK + lane % BLK
    eye = lax.broadcasted_iota(jnp.int32, (R, R), 0) == lax.broadcasted_iota(jnp.int32, (R, R), 1)
    code_col = jnp.sum(jnp.where(eye, code.astype(f32), 0.0), axis=1, keepdims=True)
    slot_col = jnp.sum(jnp.where(eye, slots.astype(f32), 0.0), axis=1, keepdims=True)
    picks = (lax.broadcasted_iota(jnp.int32, (S, R), 0) == code).astype(bf16)
    one_hot = (
        lax.broadcasted_iota(jnp.int32, (R, 128), 1).astype(f32) == slot_col
    ).astype(bf16)
    load_hid.wait()
    sbuf[:, :, D:] = (
        jnp.dot(picks, one_hot, preferred_element_type=f32).reshape(N, SL, 128).astype(bf16)
    )
    for n in range(0, D, 256):
        sbuf[:, :, n : n + 256] = (
            jnp.dot(picks, hid[:, n : n + 256], preferred_element_type=f32)
            .reshape(N, SL, 256)
            .astype(bf16)
        )
    for c in load_b:
        c.start()

    def ring(direction, d, h, arriving):
        step = d if arriving else d - 1
        s = lax.rem(z + (T - step), T) if direction == 0 else lax.rem(z + step, T)
        to = lax.rem(z + 1, T) if direction == 0 else lax.rem(z + (T - 1), T)
        rows = pl.ds(h * (R // 2), R // 2)
        src = hid.at[rows] if d == 1 else xbuf.at[s, rows]
        return pltpu.make_async_remote_copy(
            src_ref=src,
            dst_ref=xbuf.at[s, rows],
            send_sem=ring_send.at[direction, d - 1, h],
            recv_sem=ring_recv.at[direction, d - 1, h],
            device_id=(me, to),
            device_id_type=MESH,
        )

    def carries(direction, d, h):
        return d < T // 2 or (d == T // 2 and h == direction)

    def to_rep(src, dst, sems, peer):
        return pltpu.make_async_remote_copy(
            src_ref=src,
            dst_ref=dst,
            send_sem=sems.at[0],
            recv_sem=sems.at[1],
            device_id=(peer, z),
            device_id_type=MESH,
        )

    def to_tp(src, dst, sems, peer):
        return pltpu.make_async_remote_copy(
            src_ref=src,
            dst_ref=dst,
            send_sem=sems.at[0],
            recv_sem=sems.at[1],
            device_id=(me, peer),
            device_id_type=MESH,
        )

    def arrived(buf, sems):
        pltpu.make_async_copy(buf, buf, sems.at[1]).wait()

    def sent(buf, sems):
        part_of = buf.at[pl.ds(0, buf.shape[0] - 1)]
        pltpu.make_async_copy(part_of, part_of, sems.at[0]).wait()

    def ring_event(d, h):
        for direction in range(2):
            if carries(direction, d, h):
                ring(direction, d, h, True).wait_recv()
                if carries(direction, d + 1, h):
                    ring(direction, d + 1, h, False).start()

    def base_block(s, first=False):
        x = hid[...] if first else xbuf[s]
        y = jnp.dot(
            x, wcat[pl.ds(pl.multiple_of(s * D, D), D), :], preferred_element_type=f32
        )
        base[...] = y if first else base[...] + y

    def attend(chunk):
        for c in load_kv[chunk]:
            c.wait()
        C = k_hbm.shape[1]
        rs = pl.ds(chunk * RC, RC)
        position = lax.broadcasted_iota(jnp.int32, (RC, G, C), 2)
        upto = jnp.stack(
            [jnp.full((G, C), lens_ref[chunk * RC + u], jnp.int32) for u in range(RC)]
        )
        s = lax.dot_general(
            qs[rs].astype(bf16),
            kbuf[rs],
            (((2,), (2,)), ((0,), (0,))),
            preferred_element_type=f32,
        )
        s = jnp.where(position < upto, s * inverse_root, MASKED)
        m = jnp.max(s, axis=-1, keepdims=True)
        p = jnp.exp(s - m)
        l = jnp.sum(p, axis=-1, keepdims=True)
        accs[rs] = lax.dot_general(
            p.astype(bf16),
            vbuf[rs],
            (((2,), (1,)), ((0,), (0,))),
            preferred_element_type=f32,
        )
        ms[rs] = jnp.broadcast_to(m, (RC, G, HEAD_SIZE))
        ls[rs] = jnp.broadcast_to(l, (RC, G, HEAD_SIZE))

    def forward_queries():
        load_q.wait()
        for g in range(G):
            qs[:, g, :] = qin[:, g * HEAD_SIZE : (g + 1) * HEAD_SIZE].astype(f32)

    forward_queries()
    for chunk in range(EARLY):
        attend(chunk)
    pl.semaphore_wait(barrier, N - 1 + T - 1)
    for h in range(2):
        for direction in range(2):
            ring(direction, 1, h, False).start()
    for i in (2, 1, 3, 0):
        for j in (2, 1, 3, 0):
            for k in (1, 0):
                p = xs[i] + ys[j] + cs[k]
                if (i, j, k) == (0, 0, 0):
                    pltpu.make_async_copy(sbuf.at[p], rbuf.at[p], a2a_recv.at[0]).start()
                else:
                    pltpu.make_async_remote_copy(
                        src_ref=sbuf.at[p],
                        dst_ref=rbuf.at[me],
                        send_sem=a2a_send,
                        recv_sem=a2a_recv.at[i],
                        device_id=(p, z),
                        device_id_type=MESH,
                    ).start()
    for chunk in range(EARLY, KV_CHUNKS):
        attend(chunk)
    for c in load_w:
        c.wait()
    base_block(z, True)
    ring_event(1, 0)
    ring_event(1, 1)

    for c in load_a:
        c.wait()
    NG = N // NX
    for i in (0, 3, 1, 2):
        x = lax.rem(mx + (NX - i), NX)
        slabs = rbuf.at[pl.ds(x * NG, NG)]
        pltpu.make_async_copy(slabs, slabs, a2a_recv.at[i]).wait()
        rows = slabs[...].astype(f32).reshape(NG * SL, D + 128)
        hot[pl.ds(x * NG * SL, NG * SL), :] = rows[:, D:]
        y = jnp.dot(rows[:, :D].astype(bf16), acat[...], preferred_element_type=f32)
        partial = jnp.zeros((NG * SL, RANK2), f32)
        for j in range(ADP):
            partial = partial + y[:, j * RANK2 : (j + 1) * RANK2] * rows[:, D + j : D + j + 1]
        TG = T // NX
        part[pl.ds(x * TG, TG)] = partial.reshape(TG, SG, RANK2).astype(part.dtype)
        for t in range(TG):
            to = x * TG + t

            @pl.when(to != z)
            def _():
                to_tp(part.at[to], prx.at[z], rs_sem, to).start()

            @pl.when(to == z)
            def _():
                pltpu.make_async_copy(part.at[to], prx.at[to], rs_sem.at[1]).start()

    ring_event(2, 0)
    base_block(lax.rem(z + 1, T))
    base_block(lax.rem(z + T - 1, T))
    arrived(prx, rs_sem)
    total = prx[0].astype(f32)
    for t in range(1, T):
        total = total + prx[t].astype(f32)
    shr[...] = total.astype(bf16)
    for p in tp_peers:
        to_tp(shr, srx.at[z], ag_sem, p).start()
    pltpu.make_async_copy(shr, srx.at[z], ag_sem.at[1]).start()
    ring_event(2, 1)
    base_block(lax.rem(z + 2, T))
    base_block(lax.rem(z + T - 2, T))
    ring_event(3, 0)
    slabs = sbuf.at[pl.ds(0, N - 1)]
    pltpu.make_async_copy(slabs, slabs, a2a_send).wait()
    sent(part, rs_sem)
    arrived(srx, ag_sem)
    for c in load_b:
        c.wait()
    shrunk = srx[...].reshape(S, RANK2)
    masked = jnp.concatenate(
        [shrunk * hot[:, j : j + 1].astype(bf16) for j in range(ADP)], axis=1
    )
    delta = ADAPTER_SCALE * jnp.dot(masked, bcat[...], preferred_element_type=f32)
    dsend[...] = delta.reshape(N, SL, 2 * W).astype(bf16)
    for p in rep_peers:
        to_rep(dsend.at[p], drx.at[me], ret_sem, p).start()
    pltpu.make_async_copy(dsend.at[me], drx.at[me], ret_sem.at[1]).start()
    ring_event(3, 1)
    base_block(lax.rem(z + 3, T))
    base_block(lax.rem(z + T - 3, T))
    for h in range(2):
        ring_event(T // 2, h)
    base_block(lax.rem(z + T // 2, T))
    for h in range(2):
        for direction in range(2):
            for d in range(1, T // 2 + 1):
                if carries(direction, d, h):
                    ring(direction, d, h, False).wait_send()
    sent(srx, ag_sem)
    arrived(drx, ret_sem)

    spread = (
        lax.broadcasted_iota(jnp.int32, (R, S), 1).astype(f32) == code_col
    ).astype(bf16)
    got = drx[...].astype(f32).reshape(S, 2 * W).astype(bf16)
    fresh = (base[...] + jnp.dot(spread, got, preferred_element_type=f32)).astype(bf16)
    nk_ref[...] = fresh[:, :W]
    nv_ref[...] = fresh[:, W:]
    fresh = fresh.astype(f32)
    base[...] = fresh
    nk = fresh[:, :W].reshape(R, 1, W)
    nv = fresh[:, W:].reshape(R, 1, W)
    own = jnp.sum(qs[...] * nk, axis=-1, keepdims=True) * inverse_root
    m_c = ms[...]
    top = jnp.maximum(m_c, own)
    a_c = jnp.exp(m_c - top)
    a_o = jnp.exp(own - top)
    inv = 1.0 / (ls[...] * a_c + a_o)
    w_o = (a_o * inv).astype(bf16).astype(f32)
    accs[...] = accs[...] * (a_c * inv) + w_o * nv
    for g in range(G):
        ctx_ref[:, g * HEAD_SIZE : (g + 1) * HEAD_SIZE] = accs[:, g, :].astype(bf16)

    sent(dsend, ret_sem)


def put_out(a_ref, b_ref, c_ref, a_out, b_out, c_out, sem):
    copies = [
        pltpu.make_async_copy(src, dst, sem.at[i])
        for i, (src, dst) in enumerate(((c_ref, c_out), (a_ref, a_out), (b_ref, b_out)))
    ]
    for c in copies:
        c.start()
    for c in copies:
        c.wait()


def shards(
    hidden_in,
    queries,
    cache_keys,
    cached_value_rows,
    cache_lengths,
    base_key_matrix,
    base_value_matrix,
    shrink_weights,
    pooled_up_weights,
    block_owner,
    block_slot,
):
    N, T = lax.axis_size("rep"), lax.axis_size("tp")
    R, D = hidden_in.shape
    C = cache_keys.shape[1]
    W = base_key_matrix.shape[1]
    G = queries.shape[1] // HEAD_SIZE
    ADP, _, RANK2 = shrink_weights.shape
    SL = CAP * BLK
    S = N * SL
    f32, bf16 = jnp.float32, jnp.bfloat16
    hbm = pl.BlockSpec(memory_space=pltpu.HBM)
    vmem = pl.BlockSpec(memory_space=pltpu.VMEM)
    dma = pltpu.SemaphoreType.DMA
    held = pl.pallas_call(
        functools.partial(kernel, N, T),
        out_shape=(
            jax.ShapeDtypeStruct((R, W), bf16),
            jax.ShapeDtypeStruct((R, W), bf16),
            jax.ShapeDtypeStruct((R, G * HEAD_SIZE), bf16),
        ),
        in_specs=[hbm] * 11,
        out_specs=(vmem, vmem, vmem),
        scratch_shapes=[
            pltpu.SMEM((R,), jnp.int32),
            pltpu.SMEM((R // BLK,), jnp.int32),
            pltpu.SMEM((R // BLK,), jnp.int32),
            pltpu.VMEM((R, D), bf16),
            pltpu.VMEM((R, G * HEAD_SIZE), bf16),
            pltpu.VMEM((R, C, W), bf16),
            pltpu.VMEM((R, C, W), bf16),
            pltpu.VMEM((T * D, 2 * W), bf16),
            pltpu.VMEM((D, ADP * RANK2), bf16),
            pltpu.VMEM((ADP * RANK2, 2 * W), bf16),
            pltpu.VMEM((T, R, D), bf16),
            pltpu.VMEM((N, SL, D + 128), bf16),
            pltpu.VMEM((N, SL, D + 128), bf16),
            pltpu.VMEM((T, S // T, RANK2), bf16),
            pltpu.VMEM((T, S // T, RANK2), bf16),
            pltpu.VMEM((S // T, RANK2), bf16),
            pltpu.VMEM((T, S // T, RANK2), bf16),
            pltpu.VMEM((N, SL, 2 * W), bf16),
            pltpu.VMEM((N, SL, 2 * W), bf16),
            pltpu.VMEM((R, G, HEAD_SIZE), f32),
            pltpu.VMEM((R, G, HEAD_SIZE), f32),
            pltpu.VMEM((R, G, HEAD_SIZE), f32),
            pltpu.VMEM((R, G, HEAD_SIZE), f32),
            pltpu.VMEM((R, 2 * W), f32),
            pltpu.VMEM((S, 128), f32),
            dma((7 + 3 * ADP,)),
            dma((2, KV_CHUNKS)),
            dma(()),
            dma((4,)),
            dma((2, T // 2, 2)),
            dma((2, T // 2, 2)),
            dma((2,)),
            dma((2,)),
            dma((2,)),
        ],
        compiler_params=pltpu.CompilerParams(
            collective_id=0, has_side_effects=True, vmem_limit_bytes=VMEM_LIMIT
        ),
    )(
        *(
            pltpu.with_memory_space_constraint(x, pltpu.HBM)
            for x in (
                cache_lengths,
                block_owner[:, 0],
                block_slot,
                hidden_in,
                queries,
                cache_keys,
                cached_value_rows,
                base_key_matrix,
                base_value_matrix,
                shrink_weights,
                pooled_up_weights,
            )
        )
    )
    return pl.pallas_call(
        put_out,
        out_shape=tuple(jax.ShapeDtypeStruct(h.shape, h.dtype) for h in held),
        in_specs=[vmem] * 3,
        out_specs=(pl.BlockSpec(memory_space=pltpu.HBM),) * 3,
        scratch_shapes=[dma((3,))],
        compiler_params=pltpu.CompilerParams(vmem_limit_bytes=1024 * 1024),
    )(*held)


def solution(mesh):
    return jax.shard_map(
        shards,
        mesh=mesh,
        in_specs=(
            P("rep", "tp"),
            P("rep", "tp"),
            P("rep", None, "tp"),
            P("rep", None, "tp"),
            P("rep"),
            P(None, "tp"),
            P(None, "tp"),
            P("rep", "tp", None),
            P("rep", None, None, "tp"),
            P("rep", None),
            P("rep"),
        ),
        out_specs=(P("rep", "tp"), P("rep", "tp"), P("rep", "tp")),
        check_vma=False,
    )
```

time: 64.9 us -> 37.8 us (0.58)
  Pallas kernels: 52.9 us -> 37.1 us
  local copies, waits for them, and re-layouts: 11 us -> 0 us
    pallas_call x1, Pallas kernels: 52.9 us -> 36.4 us  [shards(): pl.pallas_call(functools.partial(kernel, N, T), out_shape=(jax.ShapeDtype...]
    unnamed x21 -> x0, local copies, waits for them, and re-layouts: 11 us -> none
    pallas_call x0 -> x1, Pallas kernels: none -> 0.71 us  [shards(): pl.pallas_call(put_out, out_shape=tuple((jax.ShapeDtypeStruct(h.shape, h....]
where the time goes in v2:
time: 37.8 us; the launch traced here: 37.7 us
  Pallas kernels  37.1 us (98%)
  between operations  0.64 us (2%)
    pallas_call x1, Pallas kernels, shards(): pl.pallas_call(functools.partial(kernel, N, T), out_shape=(jax.ShapeDtype...  36.4 us

profile of v2, /device:TPU:1, one launch (start us, length us, event | category | flops | bytes accessed | tf_op | source)
XLA Modules:
  0.0 37.7 jit_solution(14214138152343927506)
XLA Ops:
  0.6 36.4 %shard_map.130 = (bf16[96,128]{1,0:T(8,128)(2,1)S(1)}, bf16[96,128]{1,0:T(8,128)(2,1)S(1)}, bf16[96,1024]{1,0:T(8,128)(2,1)S(1)}) custom-call(s32[96]{0:T(128)} %lens_hbm.1, s32[24]{0:T(128)} %bitcast.1, s32[24]{0:T(128)} %slot_hbm.1, bf16[96,1024]{1,0:T(8,128)(2,1)} %hid_hbm.1, bf16[96,1024]{1,0:T(8,128)(2,1)} %q_hbm.1, bf16[96,128,128]{2,1,0:T(8,128)(2,1)} %k_hbm.1, ...), custom_call_target="tpu_custom_call" | custom-call | tf_op jit(solution)/shard_map/pallas_call | solution.py:443
  37.0 0.7 %shard_map.131 = (bf16[96,128]{1,0:T(8,128)(2,1)}, bf16[96,128]{1,0:T(8,128)(2,1)}, bf16[96,1024]{1,0:T(8,128)(2,1)}) custom-call(bf16[96,128]{1,0:T(8,128)(2,1)S(1)} %get-tuple-element.6.a_ref, bf16[96,128]{1,0:T(8,128)(2,1)S(1)} %get-tuple-element.7.b_ref, bf16[96,1024]{1,0:T(8,128)(2,1)S(1)} %get-tuple-element.8.c_ref), custom_call_target="tpu_custom_call" | custom-call | tf_op jit(solution)/shard_map/pallas_call | solution.py:509

commit v3 on v2

--- a/solution.py
+++ b/solution.py
@@ -13,7 +13,6 @@
 MASKED = -1e30
 MESH = pl.DeviceIdType.MESH
 KV_CHUNKS = 6
-EARLY = 1
 VMEM_LIMIT = 40 * 1024 * 1024
 
 
@@ -59,6 +58,9 @@
     accs,
     base,
     hot,
+    acc_g,
+    m_g,
+    l_g,
     load_sem,
     kv_sem,
     a2a_send,
@@ -66,7 +68,8 @@
     ring_send,
     ring_recv,
     rs_sem,
-    ag_sem,
+    ag_send,
+    ag_recv,
     ret_sem,
 ):
     f32, bf16 = jnp.float32, jnp.bfloat16
@@ -101,6 +104,10 @@
         if (i, j, k) != (0, 0, 0)
     ]
     tp_peers = [lax.rem(z + i, T) for i in far(T) if i]
+    for p in tp_peers:
+        pl.semaphore_signal(barrier, 1, device_id=(me, p), device_id_type=MESH)
+    for p in rep_peers:
+        pl.semaphore_signal(barrier, 1, device_id=(p, z), device_id_type=MESH)
     load_hid = pltpu.make_async_copy(hid_hbm, hid, load_sem.at[0])
     load_q = pltpu.make_async_copy(q_hbm, qin, load_sem.at[1])
     load_ids = [
@@ -112,10 +119,6 @@
     for c in load_ids:
         c.start()
     load_q.start()
-    for p in tp_peers:
-        pl.semaphore_signal(barrier, 1, device_id=(me, p), device_id_type=MESH)
-    for p in rep_peers:
-        pl.semaphore_signal(barrier, 1, device_id=(p, z), device_id_type=MESH)
     load_a = [
         pltpu.make_async_copy(
             a_hbm.at[j], acat.at[:, pl.ds(j * RANK2, RANK2)], load_sem.at[2 + j]
@@ -279,14 +282,11 @@
         for g in range(G):
             qs[:, g, :] = qin[:, g * HEAD_SIZE : (g + 1) * HEAD_SIZE].astype(f32)
 
-    forward_queries()
-    for chunk in range(EARLY):
-        attend(chunk)
     pl.semaphore_wait(barrier, N - 1 + T - 1)
     for h in range(2):
         for direction in range(2):
             ring(direction, 1, h, False).start()
-    for i in (2, 1, 3, 0):
+    for i in (0, 2, 1, 3):
         for j in (2, 1, 3, 0):
             for k in (1, 0):
                 p = xs[i] + ys[j] + cs[k]
@@ -301,28 +301,33 @@
                         device_id=(p, z),
                         device_id_type=MESH,
                     ).start()
-    for chunk in range(EARLY, KV_CHUNKS):
+    forward_queries()
+    for chunk in range(KV_CHUNKS):
         attend(chunk)
     for c in load_w:
         c.wait()
     base_block(z, True)
-    ring_event(1, 0)
-    ring_event(1, 1)
-
     for c in load_a:
         c.wait()
     NG = N // NX
-    for i in (0, 3, 1, 2):
-        x = lax.rem(mx + (NX - i), NX)
+    GR = NG * SL
+    TG = T // NX
+    odd = lax.rem(mx, 2)
+    groups = [0, 2, 1 + 2 * odd, 3 - 2 * odd]
+
+    def sender_x(i):
+        return lax.rem(mx + (NX - i), NX)
+
+    def shrink(i):
+        x = sender_x(i)
         slabs = rbuf.at[pl.ds(x * NG, NG)]
         pltpu.make_async_copy(slabs, slabs, a2a_recv.at[i]).wait()
-        rows = slabs[...].astype(f32).reshape(NG * SL, D + 128)
-        hot[pl.ds(x * NG * SL, NG * SL), :] = rows[:, D:]
+        rows = slabs[...].astype(f32).reshape(GR, D + 128)
+        hot[x] = rows[:, D:]
         y = jnp.dot(rows[:, :D].astype(bf16), acat[...], preferred_element_type=f32)
-        partial = jnp.zeros((NG * SL, RANK2), f32)
+        partial = jnp.zeros((GR, RANK2), f32)
         for j in range(ADP):
             partial = partial + y[:, j * RANK2 : (j + 1) * RANK2] * rows[:, D + j : D + j + 1]
-        TG = T // NX
         part[pl.ds(x * TG, TG)] = partial.reshape(TG, SG, RANK2).astype(part.dtype)
         for t in range(TG):
             to = x * TG + t
@@ -335,39 +340,71 @@
             def _():
                 pltpu.make_async_copy(part.at[to], prx.at[to], rs_sem.at[1]).start()
 
+    def expand(i):
+        x = sender_x(i)
+        slabs = srx.at[pl.ds(x * TG, TG)]
+        pltpu.make_async_copy(slabs, slabs, ag_recv.at[i]).wait()
+        shrunk = slabs[...].reshape(GR, RANK2)
+        hots = hot[x]
+        masked = jnp.concatenate(
+            [shrunk * hots[:, j : j + 1].astype(bf16) for j in range(ADP)], axis=1
+        )
+        delta = ADAPTER_SCALE * jnp.dot(masked, bcat[...], preferred_element_type=f32)
+        dsend[pl.ds(x * NG, NG)] = delta.reshape(NG, SL, 2 * W).astype(bf16)
+        for j in (2, 1, 3, 0):
+            for k in (1, 0):
+                p = x * NG + ys[j] + cs[k]
+                if not isinstance(i, int) or i != 0 or (j, k) != (0, 0):
+                    to_rep(dsend.at[p], drx.at[me], ret_sem, p).start()
+                else:
+                    pltpu.make_async_copy(dsend.at[p], drx.at[p], ret_sem.at[1]).start()
+
+    ring_event(1, 0)
+    ring_event(1, 1)
+    shrink(groups[0])
+    shrink(groups[1])
+    shrink(groups[2])
+    shrink(groups[3])
     ring_event(2, 0)
     base_block(lax.rem(z + 1, T))
     base_block(lax.rem(z + T - 1, T))
+    for src, dst in ((accs, acc_g), (ms, m_g), (ls, l_g)):
+        for g in range(G):
+            dst[g] = src[:, g, :]
     arrived(prx, rs_sem)
     total = prx[0].astype(f32)
     for t in range(1, T):
         total = total + prx[t].astype(f32)
     shr[...] = total.astype(bf16)
+    mine = lax.rem(mx + (NX - z // TG), NX)
     for p in tp_peers:
-        to_tp(shr, srx.at[z], ag_sem, p).start()
-    pltpu.make_async_copy(shr, srx.at[z], ag_sem.at[1]).start()
+        pltpu.make_async_remote_copy(
+            src_ref=shr,
+            dst_ref=srx.at[z],
+            send_sem=ag_send,
+            recv_sem=ag_recv.at[mine],
+            device_id=(me, p),
+            device_id_type=MESH,
+        ).start()
+    pltpu.make_async_copy(shr, srx.at[z], ag_recv.at[mine]).start()
     ring_event(2, 1)
     base_block(lax.rem(z + 2, T))
     base_block(lax.rem(z + T - 2, T))
+    for c in load_b:
+        c.wait()
     ring_event(3, 0)
+    expand(groups[0])
+    expand(groups[1])
+    expand(groups[2])
+    expand(groups[3])
+    ring_event(3, 1)
+    base_block(lax.rem(z + 3, T))
+    base_block(lax.rem(z + T - 3, T))
     slabs = sbuf.at[pl.ds(0, N - 1)]
     pltpu.make_async_copy(slabs, slabs, a2a_send).wait()
     sent(part, rs_sem)
-    arrived(srx, ag_sem)
-    for c in load_b:
-        c.wait()
-    shrunk = srx[...].reshape(S, RANK2)
-    masked = jnp.concatenate(
-        [shrunk * hot[:, j : j + 1].astype(bf16) for j in range(ADP)], axis=1
-    )
-    delta = ADAPTER_SCALE * jnp.dot(masked, bcat[...], preferred_element_type=f32)
-    dsend[...] = delta.reshape(N, SL, 2 * W).astype(bf16)
-    for p in rep_peers:
-        to_rep(dsend.at[p], drx.at[me], ret_sem, p).start()
-    pltpu.make_async_copy(dsend.at[me], drx.at[me], ret_sem.at[1]).start()
-    ring_event(3, 1)
-    base_block(lax.rem(z + 3, T))
-    base_block(lax.rem(z + T - 3, T))
+    slabs = srx.at[pl.ds(0, T - 1)]
+    pltpu.make_async_copy(slabs, slabs, ag_send).wait()
     for h in range(2):
         ring_event(T // 2, h)
     base_block(lax.rem(z + T // 2, T))
@@ -376,7 +413,6 @@
             for d in range(1, T // 2 + 1):
                 if carries(direction, d, h):
                     ring(direction, d, h, False).wait_send()
-    sent(srx, ag_sem)
     arrived(drx, ret_sem)
 
     spread = (
@@ -386,21 +422,20 @@
     fresh = (base[...] + jnp.dot(spread, got, preferred_element_type=f32)).astype(bf16)
     nk_ref[...] = fresh[:, :W]
     nv_ref[...] = fresh[:, W:]
-    fresh = fresh.astype(f32)
-    base[...] = fresh
-    nk = fresh[:, :W].reshape(R, 1, W)
-    nv = fresh[:, W:].reshape(R, 1, W)
-    own = jnp.sum(qs[...] * nk, axis=-1, keepdims=True) * inverse_root
-    m_c = ms[...]
-    top = jnp.maximum(m_c, own)
-    a_c = jnp.exp(m_c - top)
-    a_o = jnp.exp(own - top)
-    inv = 1.0 / (ls[...] * a_c + a_o)
-    w_o = (a_o * inv).astype(bf16).astype(f32)
-    accs[...] = accs[...] * (a_c * inv) + w_o * nv
+    nk = fresh[:, :W].astype(f32)
+    nv = fresh[:, W:].astype(f32)
     for g in range(G):
-        ctx_ref[:, g * HEAD_SIZE : (g + 1) * HEAD_SIZE] = accs[:, g, :].astype(bf16)
-
+        q = qin[:, g * HEAD_SIZE : (g + 1) * HEAD_SIZE].astype(f32)
+        own = jnp.sum(q * nk, axis=-1, keepdims=True) * inverse_root
+        m_c = m_g[g]
+        top = jnp.maximum(m_c, own)
+        a_c = jnp.exp(m_c - top)
+        a_o = jnp.exp(own - top)
+        inv = 1.0 / (l_g[g] * a_c + a_o)
+        w_o = (a_o * inv).astype(bf16).astype(f32)
+        ctx_ref[:, g * HEAD_SIZE : (g + 1) * HEAD_SIZE] = (
+            acc_g[g] * (a_c * inv) + w_o * nv
+        ).astype(bf16)
     sent(dsend, ret_sem)
 
 
@@ -474,7 +509,10 @@
             pltpu.VMEM((R, G, HEAD_SIZE), f32),
             pltpu.VMEM((R, G, HEAD_SIZE), f32),
             pltpu.VMEM((R, 2 * W), f32),
-            pltpu.VMEM((S, 128), f32),
+            pltpu.VMEM((4, S // 4, 128), f32),
+            pltpu.VMEM((G, R, HEAD_SIZE), f32),
+            pltpu.VMEM((G, R, HEAD_SIZE), f32),
+            pltpu.VMEM((G, R, HEAD_SIZE), f32),
             dma((7 + 3 * ADP,)),
             dma((2, KV_CHUNKS)),
             dma(()),
@@ -482,7 +520,8 @@
             dma((2, T // 2, 2)),
             dma((2, T // 2, 2)),
             dma((2,)),
-            dma((2,)),
+            dma(()),
+            dma((4,)),
             dma((2,)),
         ],
         compiler_params=pltpu.CompilerParams(

time: 37.8 us -> 36.5 us (0.966)
  Pallas kernels: 37.1 us -> 35.8 us
    pallas_call x1, Pallas kernels: 36.4 us -> 35.1 us  [shards(): pl.pallas_call(functools.partial(kernel, N, T), out_shape=(jax.ShapeDtype...]
where the time goes in v3:
time: 36.5 us
  Pallas kernels  35.8 us (98%)
  between operations  0.64 us (2%)
    pallas_call x1, Pallas kernels, shards(): pl.pallas_call(functools.partial(kernel, N, T), out_shape=(jax.ShapeDtype...  35.1 us

profile of v3, /device:TPU:1, one launch (start us, length us, event | category | flops | bytes accessed | tf_op | source)
XLA Modules:
  0.0 36.5 jit_solution(11402535283077286301)
XLA Ops:
  0.6 35.1 %shard_map.130 = (bf16[96,128]{1,0:T(8,128)(2,1)S(1)}, bf16[96,128]{1,0:T(8,128)(2,1)S(1)}, bf16[96,1024]{1,0:T(8,128)(2,1)S(1)}) custom-call(s32[96]{0:T(128)} %lens_hbm.1, s32[24]{0:T(128)} %bitcast.1, s32[24]{0:T(128)} %slot_hbm.1, bf16[96,1024]{1,0:T(8,128)(2,1)} %hid_hbm.1, bf16[96,1024]{1,0:T(8,128)(2,1)} %q_hbm.1, bf16[96,128,128]{2,1,0:T(8,128)(2,1)} %k_hbm.1, ...), custom_call_target="tpu_custom_call" | custom-call | tf_op jit(solution)/shard_map/pallas_call | solution.py:478
  35.7 0.7 %shard_map.131 = (bf16[96,128]{1,0:T(8,128)(2,1)}, bf16[96,128]{1,0:T(8,128)(2,1)}, bf16[96,1024]{1,0:T(8,128)(2,1)}) custom-call(bf16[96,128]{1,0:T(8,128)(2,1)S(1)} %get-tuple-element.6.a_ref, bf16[96,128]{1,0:T(8,128)(2,1)S(1)} %get-tuple-element.7.b_ref, bf16[96,1024]{1,0:T(8,128)(2,1)S(1)} %get-tuple-element.8.c_ref), custom_call_target="tpu_custom_call" | custom-call | tf_op jit(solution)/shard_map/pallas_call | solution.py:548

commit v4 on v3

--- a/solution.py
+++ b/solution.py
@@ -312,14 +312,11 @@
     NG = N // NX
     GR = NG * SL
     TG = T // NX
-    odd = lax.rem(mx, 2)
-    groups = [0, 2, 1 + 2 * odd, 3 - 2 * odd]
-
-    def sender_x(i):
-        return lax.rem(mx + (NX - i), NX)
-
-    def shrink(i):
-        x = sender_x(i)
+    def away(x):
+        return lax.rem(mx + (NX - x), NX)
+
+    def shrink(x):
+        i = away(x)
         slabs = rbuf.at[pl.ds(x * NG, NG)]
         pltpu.make_async_copy(slabs, slabs, a2a_recv.at[i]).wait()
         rows = slabs[...].astype(f32).reshape(GR, D + 128)
@@ -340,8 +337,8 @@
             def _():
                 pltpu.make_async_copy(part.at[to], prx.at[to], rs_sem.at[1]).start()
 
-    def expand(i):
-        x = sender_x(i)
+    def expand(x):
+        i = away(x)
         slabs = srx.at[pl.ds(x * TG, TG)]
         pltpu.make_async_copy(slabs, slabs, ag_recv.at[i]).wait()
         shrunk = slabs[...].reshape(GR, RANK2)
@@ -351,20 +348,22 @@
         )
         delta = ADAPTER_SCALE * jnp.dot(masked, bcat[...], preferred_element_type=f32)
         dsend[pl.ds(x * NG, NG)] = delta.reshape(NG, SL, 2 * W).astype(bf16)
-        for j in (2, 1, 3, 0):
+        for y in (0, 1, 3, 2):
             for k in (1, 0):
-                p = x * NG + ys[j] + cs[k]
-                if not isinstance(i, int) or i != 0 or (j, k) != (0, 0):
+                p = x * NG + y * NC + k
+
+                @pl.when(p != me)
+                def _():
                     to_rep(dsend.at[p], drx.at[me], ret_sem, p).start()
-                else:
+
+                @pl.when(p == me)
+                def _():
                     pltpu.make_async_copy(dsend.at[p], drx.at[p], ret_sem.at[1]).start()
 
     ring_event(1, 0)
     ring_event(1, 1)
-    shrink(groups[0])
-    shrink(groups[1])
-    shrink(groups[2])
-    shrink(groups[3])
+    for x in (0, 3, 1, 2):
+        shrink(x)
     ring_event(2, 0)
     base_block(lax.rem(z + 1, T))
     base_block(lax.rem(z + T - 1, T))
@@ -393,10 +392,8 @@
     for c in load_b:
         c.wait()
     ring_event(3, 0)
-    expand(groups[0])
-    expand(groups[1])
-    expand(groups[2])
-    expand(groups[3])
+    for x in (0, 3, 1, 2):
+        expand(x)
     ring_event(3, 1)
     base_block(lax.rem(z + 3, T))
     base_block(lax.rem(z + T - 3, T))

time: 36.5 us -> 35.5 us (0.973)
  Pallas kernels: 35.8 us -> 34.7 us
    pallas_call x1, Pallas kernels: 35.1 us -> 34 us  [shards(): pl.pallas_call(functools.partial(kernel, N, T), out_shape=(jax.ShapeDtype...]
where the time goes in v4:
time: 35.5 us; the launch traced here: 35.4 us
  Pallas kernels  34.7 us (98%)
  between operations  0.64 us (2%)
    pallas_call x1, Pallas kernels, shards(): pl.pallas_call(functools.partial(kernel, N, T), out_shape=(jax.ShapeDtype...  34 us

profile of v4, /device:TPU:1, one launch (start us, length us, event | category | flops | bytes accessed | tf_op | source)
XLA Modules:
  0.0 35.4 jit_solution(2784835488268434504)
XLA Ops:
  0.6 34.0 %shard_map.130 = (bf16[96,128]{1,0:T(8,128)(2,1)S(1)}, bf16[96,128]{1,0:T(8,128)(2,1)S(1)}, bf16[96,1024]{1,0:T(8,128)(2,1)S(1)}) custom-call(s32[96]{0:T(128)} %lens_hbm.1, s32[24]{0:T(128)} %bitcast.1, s32[24]{0:T(128)} %slot_hbm.1, bf16[96,1024]{1,0:T(8,128)(2,1)} %hid_hbm.1, bf16[96,1024]{1,0:T(8,128)(2,1)} %q_hbm.1, bf16[96,128,128]{2,1,0:T(8,128)(2,1)} %k_hbm.1, ...), custom_call_target="tpu_custom_call" | custom-call | tf_op jit(solution)/shard_map/pallas_call | solution.py:475
  34.7 0.7 %shard_map.131 = (bf16[96,128]{1,0:T(8,128)(2,1)}, bf16[96,128]{1,0:T(8,128)(2,1)}, bf16[96,1024]{1,0:T(8,128)(2,1)}) custom-call(bf16[96,128]{1,0:T(8,128)(2,1)S(1)} %get-tuple-element.6.a_ref, bf16[96,128]{1,0:T(8,128)(2,1)S(1)} %get-tuple-element.7.b_ref, bf16[96,1024]{1,0:T(8,128)(2,1)S(1)} %get-tuple-element.8.c_ref), custom_call_target="tpu_custom_call" | custom-call | tf_op jit(solution)/shard_map/pallas_call | solution.py:545
